TPU v7x, 512 devices: a whole 4x4x16 slice. The times are simulated.
512 devices in a mesh: ctx: 32 (over x, z_lo), tp: 16 (over y, z_hi, core).
Axes of the slice: x: 4, y: 4, z: 16 (z_hi: 2, z_lo: 8; z = z_hi * 8 + z_lo), core: 2. Of those that a mesh axis runs over, the one named last changes fastest.
Arguments:
- queries: bfloat16 [4096, 4096], P('ctx', 'tp'), may hold values from -5 to 5
- key_states: bfloat16 [4096, 4096], P('ctx', 'tp'), may hold values from -5 to 5
- value_states: bfloat16 [4096, 4096], P('ctx', 'tp'), may hold values from -6 to 6
- attn_output: bfloat16 [4096, 4096], P('ctx', 'tp'), may hold values from -6 to 6
- output_grad: bfloat16 [4096, 4096], P('ctx', 'tp'), may hold values from -6 to 6
- block_map: int32 [32, 32], replicated, may hold values from 0 to 1, as said below
- w_query: bfloat16 [8192, 4096], P('ctx', 'tp'), may hold values from -0.09375 to 0.09375
- w_key: bfloat16 [8192, 4096], P('ctx', 'tp'), may hold values from -0.09375 to 0.09375
- w_value: bfloat16 [8192, 4096], P('ctx', 'tp'), may hold values from -0.09375 to 0.09375
Outputs:
- grad_input: bfloat16 [4096, 8192], P('tp', 'ctx')
Inputs may be any that keep to these rules, and one draw needn't show every extreme that they name: block_map[i, j] is 1 wherever |i - j| <= 1; elsewhere each row is 1 on a share of its entries that differs from row to row.
All inputs are finite; a program needn't handle non-finite values.
Results may differ from a plain program's by a relative error of at most 0.014.
Values may be sent and summed in bfloat16 or wider, within the bound.
No kernel may reach another device: no remote copies, remote signals or barrier semaphores. Data moves between devices by JAX's collectives and lax.ppermute only.
A program may use at most 64 MiB of HBM per device.

v0:
```python
import math
import jax
import jax.numpy as jnp
from jax import lax
from jax.sharding import PartitionSpec as P

HD = 128
BLK = 128
NEG_FILL = -1e30


def block_mask(block_map, row_offset, row_count, col_offset, col_count):
    tiles = lax.dynamic_slice(
        block_map, (row_offset // BLK, col_offset // BLK), (row_count // BLK, col_count // BLK)
    )
    spread = jnp.broadcast_to(
        tiles[:, None, :, None], (row_count // BLK, BLK, col_count // BLK, BLK)
    )
    return spread.reshape(row_count, col_count) > 0


def resolved_rows(values):
    return lax.optimization_barrier(values.astype(jnp.bfloat16)).astype(jnp.float32)


def stat_update(state, query_heads, key_block, allowed, score_scale):
    row_max, row_sum = state
    scores = (
        jnp.einsum("qhd,khd->hqk", query_heads, key_block, preferred_element_type=jnp.float32)
        * score_scale
    )
    masked = jnp.where(allowed[None], scores, NEG_FILL)
    new_max = jnp.maximum(row_max, jnp.max(masked, axis=2))
    kept = jnp.where(allowed[None], jnp.exp(masked - new_max[:, :, None]), 0.0)
    return (new_max, row_sum * jnp.exp(row_max - new_max) + jnp.sum(kept, axis=2))


def gradient_block(
    query_heads, grad_heads, key_block, value_block, log_total, row_delta, allowed, score_scale
):
    scores = (
        jnp.einsum("qhd,khd->hqk", query_heads, key_block, preferred_element_type=jnp.float32)
        * score_scale
    )
    masked = jnp.where(allowed[None], scores, NEG_FILL)
    probs = jnp.where(allowed[None], jnp.exp(masked - log_total[:, :, None]), 0.0)
    probs_low = probs.astype(jnp.bfloat16)
    dprobs = jnp.einsum("qhd,khd->hqk", grad_heads, value_block, preferred_element_type=jnp.float32)
    score_gradient = (probs * (dprobs - row_delta[:, :, None]) * score_scale).astype(jnp.bfloat16)
    return (probs_low, score_gradient)


def per_device(
    queries, key_states, value_states, attn_output, output_grad, block_map, w_query, w_key, w_value
):
    slab_rows, width = queries.shape
    head_count = width // HD
    context_count = lax.axis_size("ctx")
    score_scale = 1.0 / math.sqrt(HD)
    row_offset = lax.axis_index("ctx") * slab_rows
    query_heads = queries.reshape(slab_rows, head_count, HD)
    grad_heads = output_grad.reshape(slab_rows, head_count, HD)
    output_heads = attn_output.reshape(slab_rows, head_count, HD)
    row_delta = jnp.sum(grad_heads.astype(jnp.float32) * output_heads.astype(jnp.float32), axis=2).T
    start_state = (
        jnp.full((head_count, slab_rows), NEG_FILL, jnp.float32),
        jnp.zeros((head_count, slab_rows), jnp.float32),
    )
    full_keys, full_values = (
        lax.all_gather(key_states, "ctx", axis=0, tiled=True),
        lax.all_gather(value_states, "ctx", axis=0, tiled=True),
    )
    group_size = min(context_count, max(1, 512 // slab_rows))
    key_span = slab_rows * group_size
    total_block_count = context_count // group_size
    key_blocks = full_keys.reshape(total_block_count, key_span, head_count, HD)
    value_blocks = full_values.reshape(total_block_count, key_span, head_count, HD)
    block_ids = jnp.arange(total_block_count, dtype=jnp.int32)

    def stat_step(state, inputs):
        key_block, block_index = inputs
        allowed = block_mask(block_map, row_offset, slab_rows, block_index * key_span, key_span)

        def stat_active_step(previous):
            return stat_update(previous, query_heads, key_block, allowed, score_scale)

        return (
            lax.cond(jnp.any(allowed), stat_active_step, lambda previous: previous, state),
            None,
        )

    (row_max, row_sum), _ = lax.scan(stat_step, start_state, (key_blocks, block_ids))
    log_total = row_max + jnp.log(row_sum)

    def back_step(dq_total, inputs):
        key_block, value_block, block_index = inputs
        allowed = block_mask(block_map, row_offset, slab_rows, block_index * key_span, key_span)

        def back_active_step(previous):
            probs_low, score_gradient = gradient_block(
                query_heads,
                grad_heads,
                key_block,
                value_block,
                log_total,
                row_delta,
                allowed,
                score_scale,
            )
            dv_part = jnp.einsum(
                "hqk,qhd->khd", probs_low, grad_heads, preferred_element_type=jnp.float32
            ).astype(jnp.bfloat16)
            dk_part = jnp.einsum(
                "hqk,qhd->khd", score_gradient, query_heads, preferred_element_type=jnp.float32
            ).astype(jnp.bfloat16)
            per_slab = jnp.einsum(
                "hqgk,gkhd->gqhd",
                score_gradient.reshape(head_count, slab_rows, group_size, slab_rows),
                key_block.reshape(group_size, slab_rows, head_count, HD),
                preferred_element_type=jnp.float32,
            )
            joined = jnp.concatenate(
                [dk_part.reshape(key_span, width), dv_part.reshape(key_span, width)], axis=1
            )
            return (previous + jnp.sum(resolved_rows(per_slab), axis=0), joined)

        def empty_step(previous):
            return (previous, jnp.zeros((key_span, 2 * width), jnp.bfloat16))

        return lax.cond(jnp.any(allowed), back_active_step, empty_step, dq_total)

    dq_total, joined_blocks = lax.scan(
        back_step,
        jnp.zeros((slab_rows, head_count, HD), jnp.float32),
        (key_blocks, value_blocks, block_ids),
    )
    local_grads = dq_total.astype(jnp.bfloat16).reshape(slab_rows, width)
    part_grads = joined_blocks.reshape(context_count * slab_rows, 2 * width)
    part_width = part_grads.shape[1]
    arrived = lax.all_to_all(
        part_grads.reshape(context_count, slab_rows, part_width),
        "ctx",
        split_axis=0,
        concat_axis=0,
        tiled=True,
    )
    finished = jnp.sum(arrived.astype(jnp.float32), axis=0).astype(jnp.bfloat16)
    own_grads = jnp.concatenate([local_grads, finished], axis=1)
    gradients = lax.all_gather(own_grads, "ctx", axis=0, tiled=True)
    projections = jnp.concatenate([w_query, w_key, w_value], axis=1)
    return lax.psum_scatter(
        lax.dot_general(
            gradients, projections, (((1,), (1,)), ((), ())), preferred_element_type=jnp.float32
        ).astype(jnp.bfloat16),
        "tp",
        scatter_dimension=0,
        tiled=True,
    )


def solution(mesh):
    return jax.shard_map(
        per_device,
        mesh=mesh,
        in_specs=(
            P("ctx", "tp"),
            P("ctx", "tp"),
            P("ctx", "tp"),
            P("ctx", "tp"),
            P("ctx", "tp"),
            P(),
            P("ctx", "tp"),
            P("ctx", "tp"),
            P("ctx", "tp"),
        ),
        out_specs=P("tp", "ctx"),
        check_vma=False,
    )
```

profile of v0, /device:TPU:2, one launch (start us, length us, event | category | flops | bytes accessed | tf_op | source)
XLA Modules:
  0.0 1083.6 jit_solution(8561882724283096852)
XLA Ops:
  8.0 1.0 copy.66
  9.1 1.0 copy.70
  10.1 0.9 copy.71
  11.1 212.4 %all-gather.4.cloned.1.call-done = bf16[4096,256]{1,0:T(8,128)(2,1)} async-done(((bf16[128,256]{1,0:T(8,128)(2,1)}), bf16[4096,256]{1,0:T(8,128)(2,1)}) %all-gather.4.cloned.1.call-update) | async-done | bytes 2097168 | tf_op jit(solution)/shard_map/all_gather | solution.py:70
  223.4 4.0 reshape.84
  227.4 2.0 copy.72
  229.5 30.8 %while.33 = (s32[]{:T(128)}, f32[2,128]{1,0:T(2,128)S(1)}, f32[2,128]{1,0:T(2,128)S(1)}, s32[8]{0:T(128)S(1)}, s32[32,32]{1,0:T(8,128)}, /*index=5*/s32[]{:T(128...) while((s32[]{:T(128)}, f32[2,128]{1,0:T(2,128)S(1)}, ...), condition=%wide.region_6.7_spmd, body=%wide.region_0.6_spmd.sunk | while | flops 34406940 | bytes 1391623 | solution.py:92
  230.6 0.8 broadcast_compare_fusion.6
  231.4 0.8 broadcast_reduce_fusion.4
  234.5 0.8 broadcast_compare_fusion.6
  235.3 0.8 broadcast_reduce_fusion.4
  238.3 0.8 broadcast_compare_fusion.6
  239.1 0.8 broadcast_reduce_fusion.4
  242.2 0.8 broadcast_compare_fusion.6
  243.0 0.8 broadcast_reduce_fusion.4
  246.0 0.8 broadcast_compare_fusion.6
  246.8 0.8 broadcast_reduce_fusion.4
  249.9 0.8 broadcast_compare_fusion.6
  250.7 0.8 broadcast_reduce_fusion.4
  253.8 0.8 broadcast_compare_fusion.6
  257.6 0.8 broadcast_compare_fusion.6
  260.3 189.8 %all-gather.6.cloned.1.call-done = bf16[4096,256]{1,0:T(8,128)(2,1)} async-done(((bf16[128,256]{1,0:T(8,128)(2,1)}), bf16[4096,256]{1,0:T(8,128)(2,1)}) %all-gather.6.cloned.1.call-update) | async-done | bytes 2097168 | tf_op jit(solution)/shard_map/all_gather | solution.py:71
  450.1 4.0 reshape.85
  454.1 3.3 copy.73
  457.5 54.5 %while.34 = (s32[]{:T(128)}, f32[128,2,128]{2,0,1:T(8,128)S(1)}, bf16[8,512,512]{2,1,0:T(8,128)(2,1)}, s32[8]{0:T(128)S(1)}, s32[32,32]{1,0:T(8,128)}, /*index=5...) while((s32[]{:T(128)}, f32[128,2,128]{2,0,1:T(8,128)S(1)}, ...), condition=%wide.region_13.14_spmd, body=%wide.region_8.13_spmd.sunk | while | flops 170721312 | bytes 8655399 | solution.py:132
  458.6 0.8 broadcast_compare_fusion.7
  460.7 2.5 conditional.5
  461.2 1.2 fusion.11
  463.4 0.8 constant_dynamic-update-slice_fusion.2
  465.4 0.8 broadcast_compare_fusion.7
  467.5 2.5 conditional.5
  468.0 1.2 fusion.11
  470.2 0.8 constant_dynamic-update-slice_fusion.2
  472.2 0.8 broadcast_compare_fusion.7
  474.3 2.5 conditional.5
  474.8 1.2 fusion.11
  477.0 0.8 constant_dynamic-update-slice_fusion.2
  479.1 0.8 broadcast_compare_fusion.7
  481.2 2.5 conditional.5
  481.6 1.2 fusion.11
  483.9 0.8 constant_dynamic-update-slice_fusion.2
  485.9 0.8 broadcast_compare_fusion.7
  488.0 2.5 conditional.5
  488.4 1.2 fusion.11
  490.7 0.8 constant_dynamic-update-slice_fusion.2
  492.7 0.8 broadcast_compare_fusion.7
  493.4 0.8 broadcast_reduce_fusion.5
  494.8 2.5 conditional.5
  495.2 1.2 fusion.11
  497.5 0.9 constant_dynamic-update-slice_fusion.2
  499.5 0.8 broadcast_compare_fusion.7
  501.6 2.5 conditional.5
  502.0 1.2 fusion.11
  504.3 0.8 constant_dynamic-update-slice_fusion.2
  506.3 0.8 broadcast_compare_fusion.7
  508.4 2.5 conditional.5
  508.8 1.2 fusion.11
  511.1 0.8 constant_dynamic-update-slice_fusion.2
  511.9 30.9 %all-to-all-start = ((bf16[32,128,512]{2,1,0:T(8,128)(2,1)}), bf16[32,128,512]{2,1,0:T(8,128)(2,1)}, u32[]{:S(2)}, u32[]{:S(2)}) async-start(bf16[32,128,512]{2,1,0:T(8,128)(2,1)} %bitcast.63), calls=%async_computation | async-start | bytes 8388608 | tf_op jit(solution)/shard_map/all_to_all | solution.py:140
  543.1 152.9 %all-to-all-done = bf16[32,128,512]{2,1,0:T(8,128)(2,1)} async-done(((bf16[32,128,512]{2,1,0:T(8,128)(2,1)}), bf16[32,128,512]{2,1,0:T(8,128)(2,1)}, u32[]{:S(2)}, u32[]{:S(2)}) %all-to-all-start) | async-done | bytes 4194336 | tf_op jit(solution)/shard_map/all_to_all | solution.py:140
  696.0 2.8 reduce_sum.43
  699.6 233.9 %all-gather.8.cloned.1.call-done = bf16[4096,768]{1,0:T(8,128)(2,1)} async-done(((bf16[128,768]{1,0:T(8,128)(2,1)}), bf16[4096,768]{1,0:T(8,128)(2,1)}) %all-gather.8.cloned.1.call-update) | async-done | bytes 6291472 | tf_op jit(solution)/shard_map/all_gather | solution.py:149
  933.5 6.0 convolution_convert_fusion.3
  939.5 137.5 %reduce-scatter.2.cloned.1.call-done = bf16[256,256]{1,0:T(8,128)(2,1)} async-done(((bf16[4096,256]{1,0:T(8,128)(2,1)}), bf16[256,256]{1,0:T(8,128)(2,1)}) %reduce-scatter.2.cloned.1.call-update) | async-done | bytes 131088 | tf_op jit(solution)/shard_map/reduce_scatter | solution.py:151
  (203 shorter events, 38.5 us)
Async XLA Ops:
  6.5 216.9 %all-gather.4.cloned.1.call-start = ((), (), s32[]{:S(2)}) async-start(), calls=%async_computation.2 | async-start | bytes 2162688 | tf_op jit(solution)/shard_map/all_gather | solution.py:70
  7.3 442.8 %all-gather.6.cloned.1.call-start = ((), (), s32[]{:S(2)}) async-start(), calls=%async_computation.3 | async-start | bytes 2162688 | tf_op jit(solution)/shard_map/all_gather | solution.py:71
  511.9 184.1 %all-to-all-start = ((bf16[32,128,512]{2,1,0:T(8,128)(2,1)}), bf16[32,128,512]{2,1,0:T(8,128)(2,1)}, u32[]{:S(2)}, u32[]{:S(2)}) async-start(bf16[32,128,512]{2,1,0:T(8,128)(2,1)} %bitcast.63), calls=%async_computation | async-start | bytes 8388608 | tf_op jit(solution)/shard_map/all_to_all | solution.py:140
  542.8 390.7 %copy-start = (bf16[256,256]{1,0:T(8,128)(2,1)S(1)}, bf16[256,256]{1,0:T(8,128)(2,1)}, u32[]{:S(2)}) copy-start(bf16[256,256]{1,0:T(8,128)(2,1)} %param.25) | copy-start | bytes 393220
  542.8 390.7 %copy-start.1 = (bf16[256,256]{1,0:T(8,128)(2,1)S(1)}, bf16[256,256]{1,0:T(8,128)(2,1)}, u32[]{:S(2)}) copy-start(bf16[256,256]{1,0:T(8,128)(2,1)} %param.24) | copy-start | bytes 393220
  542.8 390.7 %copy-start.2 = (bf16[256,256]{1,0:T(8,128)(2,1)S(1)}, bf16[256,256]{1,0:T(8,128)(2,1)}, u32[]{:S(2)}) copy-start(bf16[256,256]{1,0:T(8,128)(2,1)} %param.23) | copy-start | bytes 393220
  542.8 390.7 %all-gather.8.cloned.1.call-start = ((), (), s32[]{:S(2)}) async-start(), calls=%async_computation.4 | async-start | bytes 6488064 | tf_op jit(solution)/shard_map/all_gather | solution.py:149
  699.6 377.5 %reduce-scatter.2.cloned.1.call-start = ((), (), s32[]{:S(2)}) async-start(), calls=%async_computation.5 | async-start | bytes 2228224 | tf_op jit(solution)/shard_map/reduce_scatter | solution.py:151
Sparse Core Ops, SparseCore 0:
  9.4 213.9 all-gather.3
  225.5 224.5 all-gather.5
  699.7 233.7 all-gather.7
  939.6 137.3 reduce-scatter.1
where the time goes:
time: 1090 us; the launch traced here: 1080 us
  waiting for transfers between devices  928 us (85%)
  local copies, waits for them, and re-layouts  35.5 us (3%)
  starting transfers between devices  31 us (3%)
  other arithmetic  30.4 us (3%)
  matrix products  25.4 us (2%)
  loops' own time  20.1 us (2%)
  between operations  13.3 us (1%)
    all_gather x1, waiting for transfers between devices, per_device(): gradients = lax.all_gather(own_grads, 'ctx', axis=0, tiled=True)  234 us
    all_gather x1, waiting for transfers between devices, per_device(): lax.all_gather(key_states, 'ctx', axis=0, tiled=True)  212 us
    all_gather x1, waiting for transfers between devices, per_device(): lax.all_gather(value_states, 'ctx', axis=0, tiled=True)  190 us
    all_to_all x1, waiting for transfers between devices, per_device(): lax.all_to_all(part_grads.reshape(context_count, slab_rows, part_width),...  153 us
    reduce_scatter x1, waiting for transfers between devices, per_device(): lax.psum_scatter(lax.dot_general(gradients, projections, (((1,), (1,)), (...  138 us
    all_to_all x1, starting transfers between devices, per_device(): lax.all_to_all(part_grads.reshape(context_count, slab_rows, part_width),...  30.9 us
  transfers between devices with their start and end apart: 5, of which 5 were waited for; matrix products, arithmetic and copies ran while one was open for 3% of the time, Pallas kernels for 0%

commit v1 on v0

--- a/solution.py
+++ b/solution.py
@@ -67,7 +67,12 @@
         jnp.zeros((head_count, slab_rows), jnp.float32),
     )
     full_keys, full_values = (
-        lax.all_gather(key_states, "ctx", axis=0, tiled=True),
+        jnp.concatenate(
+            lax.all_to_all(
+                jnp.stack([key_states for _ in range(lax.psum(1, "ctx"))], 0), "ctx", 0, 0
+            ),
+            0,
+        ),
         lax.all_gather(value_states, "ctx", axis=0, tiled=True),
     )
     group_size = min(context_count, max(1, 512 // slab_rows))

time: 1090 us -> 940 us (0.86)
  the two profiles are of different devices: /device:TPU:2 before, /device:TPU:4 now
where the time goes in v1:
time: 940 us; the launch traced here: 938 us
  waiting for transfers between devices  767 us (82%)
  local copies, waits for them, and re-layouts  41.4 us (4%)
  starting transfers between devices  38 us (4%)
  other arithmetic  31.5 us (3%)
  matrix products  25.4 us (3%)
  loops' own time  21.7 us (2%)
  between operations  13.3 us (1%)
    all_gather x1, waiting for transfers between devices, per_device(): gradients = lax.all_gather(own_grads, 'ctx', axis=0, tiled=True)  235 us
    all_gather x1, waiting for transfers between devices, per_device(): lax.all_gather(value_states, 'ctx', axis=0, tiled=True)  233 us
    all_to_all x1, waiting for transfers between devices, per_device(): lax.all_to_all(part_grads.reshape(context_count, slab_rows, part_width),...  160 us
    reduce_scatter x1, waiting for transfers between devices, per_device(): lax.psum_scatter(lax.dot_general(gradients, projections, (((1,), (1,)), (...  138 us
    all_to_all x1, starting transfers between devices, per_device(): lax.all_to_all(part_grads.reshape(context_count, slab_rows, part_width),...  22.1 us
  transfers between devices with their start and end apart: 5, of which 4 were waited for; matrix products, arithmetic and copies ran while one was open for 1% of the time, Pallas kernels for 0%

profile of v1, /device:TPU:4, one launch (start us, length us, event | category | flops | bytes accessed | tf_op | source)
XLA Modules:
  0.0 938.4 jit_solution(3557537594540027605)
XLA Ops:
  6.5 0.9 copy.67
  7.5 1.8 stack.2
  9.3 15.8 %all-to-all-start = ((bf16[32,128,256]{1,2,0:T(8,128)(2,1)}), bf16[32,128,256]{1,2,0:T(8,128)(2,1)S(1)}, u32[]{:S(2)}, u32[]{:S(2)}) async-start(bf16[32,128,256]{1,2,0:T(8,128)(2,1)} %stack.2), calls=%async_computation | async-start | bytes 4194304 | tf_op jit(solution)/shard_map/all_to_all | solution.py:71
  26.4 233.4 %all-gather.3.cloned.1.call-done = bf16[4096,256]{1,0:T(8,128)(2,1)} async-done(((bf16[128,256]{1,0:T(8,128)(2,1)}), bf16[4096,256]{1,0:T(8,128)(2,1)}) %all-gather.3.cloned.1.call-update) | async-done | bytes 2097168 | tf_op jit(solution)/shard_map/all_gather | solution.py:76
  259.9 4.0 reshape.82
  263.8 3.3 copy.76
  267.2 2.7 copy.68
  269.9 4.4 reshape_reshape.6
  274.2 3.5 copy.75
  277.7 32.7 %while.33 = (s32[]{:T(128)}, f32[2,128]{1,0:T(2,128)S(1)}, f32[2,128]{1,0:T(2,128)S(1)}, s32[8]{0:T(128)S(1)}, s32[32,32]{1,0:T(8,128)}, /*index=5*/s32[]{:T(128...) while((s32[]{:T(128)}, f32[2,128]{1,0:T(2,128)S(1)}, ...), condition=%wide.region_6.7_spmd, body=%wide.region_0.6_spmd.sunk | while | flops 34406940 | bytes 1391623 | solution.py:97
  279.1 0.8 broadcast_compare_fusion.6
  279.8 0.8 broadcast_reduce_fusion.4
  283.1 0.8 broadcast_compare_fusion.6
  283.9 0.8 broadcast_reduce_fusion.4
  287.2 0.8 broadcast_compare_fusion.6
  288.0 0.8 broadcast_reduce_fusion.4
  291.3 0.8 broadcast_compare_fusion.6
  292.1 0.8 broadcast_reduce_fusion.4
  295.4 0.8 broadcast_compare_fusion.6
  296.2 0.8 broadcast_reduce_fusion.4
  300.3 0.8 broadcast_reduce_fusion.4
  304.4 0.8 broadcast_reduce_fusion.4
  308.5 0.8 broadcast_reduce_fusion.4
  310.5 56.4 %while.34 = (s32[]{:T(128)}, f32[128,2,128]{2,0,1:T(8,128)S(1)}, bf16[8,512,512]{2,1,0:T(8,128)(2,1)}, s32[8]{0:T(128)S(1)}, s32[32,32]{1,0:T(8,128)}, /*index=5...) while((s32[]{:T(128)}, f32[128,2,128]{2,0,1:T(8,128)S(1)}, ...), condition=%wide.region_13.14_spmd, body=%wide.region_8.13_spmd.sunk | while | flops 170721312 | bytes 8655399 | solution.py:137
  311.8 0.8 broadcast_compare_fusion.7
  312.6 0.8 broadcast_reduce_fusion.5
  314.1 2.5 conditional.5
  314.5 1.2 fusion.11
  316.8 0.8 constant_dynamic-update-slice_fusion.2
  318.9 0.8 broadcast_compare_fusion.7
  319.7 0.8 broadcast_reduce_fusion.5
  321.1 2.5 conditional.5
  321.5 1.2 fusion.11
  323.8 0.8 constant_dynamic-update-slice_fusion.2
  326.7 0.8 broadcast_reduce_fusion.5
  328.2 2.5 conditional.5
  328.6 1.2 fusion.11
  330.9 0.8 constant_dynamic-update-slice_fusion.2
  333.8 0.8 broadcast_reduce_fusion.5
  335.2 2.5 conditional.5
  335.6 1.2 fusion.11
  337.9 0.8 constant_dynamic-update-slice_fusion.2
  340.8 0.8 broadcast_reduce_fusion.5
  342.3 2.5 conditional.5
  342.7 1.2 fusion.11
  345.0 0.8 constant_dynamic-update-slice_fusion.2
  347.9 0.8 broadcast_reduce_fusion.5
  349.3 2.5 conditional.5
  349.7 1.2 fusion.11
  352.0 0.8 constant_dynamic-update-slice_fusion.2
  354.9 0.8 broadcast_reduce_fusion.5
  356.4 2.5 conditional.5
  356.8 1.2 fusion.11
  359.1 0.8 constant_dynamic-update-slice_fusion.2
  362.0 0.8 broadcast_reduce_fusion.5
  363.4 2.5 conditional.5
  363.8 1.2 fusion.11
  366.1 0.8 constant_dynamic-update-slice_fusion.2
  367.0 22.1 %all-to-all-start.1 = ((bf16[32,128,512]{2,1,0:T(8,128)(2,1)}), bf16[32,128,512]{2,1,0:T(8,128)(2,1)}, u32[]{:S(2)}, u32[]{:S(2)}) async-start(bf16[32,128,512]{2,1,0:T(8,128)(2,1)} %bitcast.65), calls=%async_computation.1 | async-start | bytes 8388608 | tf_op jit(solution)/shard_map/all_to_all | solution.py:145
  389.4 160.4 %all-to-all-done.1 = bf16[32,128,512]{2,1,0:T(8,128)(2,1)} async-done(((bf16[32,128,512]{2,1,0:T(8,128)(2,1)}), bf16[32,128,512]{2,1,0:T(8,128)(2,1)}, u32[]{:S(2)}, u32[]{:S(2)}) %all-to-all-start.1) | async-done | bytes 4194336 | tf_op jit(solution)/shard_map/all_to_all | solution.py:145
  549.8 2.8 reduce_sum.43
  553.3 234.8 %all-gather.5.cloned.1.call-done = bf16[4096,768]{1,0:T(8,128)(2,1)} async-done(((bf16[128,768]{1,0:T(8,128)(2,1)}), bf16[4096,768]{1,0:T(8,128)(2,1)}) %all-gather.5.cloned.1.call-update) | async-done | bytes 6291472 | tf_op jit(solution)/shard_map/all_gather | solution.py:154
  788.2 6.0 convolution_convert_fusion.3
  794.2 137.7 %reduce-scatter.2.cloned.1.call-done = bf16[256,256]{1,0:T(8,128)(2,1)} async-done(((bf16[4096,256]{1,0:T(8,128)(2,1)}), bf16[256,256]{1,0:T(8,128)(2,1)}) %reduce-scatter.2.cloned.1.call-update) | async-done | bytes 131088 | tf_op jit(solution)/shard_map/reduce_scatter | solution.py:156
  (211 shorter events, 39.3 us)
Async XLA Ops:
  9.3 16.6 %copy-start.1 = (bf16[128,256]{1,0:T(8,128)(2,1)S(1)}, bf16[128,256]{1,0:T(8,128)(2,1)}, u32[]{:S(2)}) copy-start(bf16[128,256]{1,0:T(8,128)(2,1)} %param.17) | copy-start | bytes 196612
  9.3 16.8 %copy-start.2 = (bf16[128,256]{1,0:T(8,128)(2,1)S(1)}, bf16[128,256]{1,0:T(8,128)(2,1)}, u32[]{:S(2)}) copy-start(bf16[128,256]{1,0:T(8,128)(2,1)} %param.21) | copy-start | bytes 196612
  9.3 17.0 %copy-start = (bf16[128,256]{1,0:T(8,128)(2,1)S(1)}, bf16[128,256]{1,0:T(8,128)(2,1)}, u32[]{:S(2)}) copy-start(bf16[128,256]{1,0:T(8,128)(2,1)} %param.20) | copy-start | bytes 196612
  9.3 257.8 %all-to-all-start = ((bf16[32,128,256]{1,2,0:T(8,128)(2,1)}), bf16[32,128,256]{1,2,0:T(8,128)(2,1)S(1)}, u32[]{:S(2)}, u32[]{:S(2)}) async-start(bf16[32,128,256]{1,2,0:T(8,128)(2,1)} %stack.2), calls=%async_computation | async-start | bytes 4194304 | tf_op jit(solution)/shard_map/all_to_all | solution.py:71
  25.1 234.7 %all-gather.3.cloned.1.call-start = ((), (), s32[]{:S(2)}) async-start(), calls=%async_computation.3 | async-start | bytes 2162688 | tf_op jit(solution)/shard_map/all_gather | solution.py:76
  367.0 182.8 %all-to-all-start.1 = ((bf16[32,128,512]{2,1,0:T(8,128)(2,1)}), bf16[32,128,512]{2,1,0:T(8,128)(2,1)}, u32[]{:S(2)}, u32[]{:S(2)}) async-start(bf16[32,128,512]{2,1,0:T(8,128)(2,1)} %bitcast.65), calls=%async_computation.1 | async-start | bytes 8388608 | tf_op jit(solution)/shard_map/all_to_all | solution.py:145
  389.1 399.1 %all-gather.5.cloned.1.call-start = ((), (), s32[]{:S(2)}) async-start(), calls=%async_computation.4 | async-start | bytes 6488064 | tf_op jit(solution)/shard_map/all_gather | solution.py:154
  389.4 398.8 %copy-start.3 = (bf16[256,256]{1,0:T(8,128)(2,1)S(1)}, bf16[256,256]{1,0:T(8,128)(2,1)}, u32[]{:S(2)}) copy-start(bf16[256,256]{1,0:T(8,128)(2,1)} %param.25) | copy-start | bytes 393220
  389.4 398.8 %copy-start.4 = (bf16[256,256]{1,0:T(8,128)(2,1)S(1)}, bf16[256,256]{1,0:T(8,128)(2,1)}, u32[]{:S(2)}) copy-start(bf16[256,256]{1,0:T(8,128)(2,1)} %param.24) | copy-start | bytes 393220
  389.4 398.8 %copy-start.5 = (bf16[256,256]{1,0:T(8,128)(2,1)S(1)}, bf16[256,256]{1,0:T(8,128)(2,1)}, u32[]{:S(2)}) copy-start(bf16[256,256]{1,0:T(8,128)(2,1)} %param.23) | copy-start | bytes 393220
  553.3 378.6 %reduce-scatter.2.cloned.1.call-start = ((), (), s32[]{:S(2)}) async-start(), calls=%async_computation.5 | async-start | bytes 2228224 | tf_op jit(solution)/shard_map/reduce_scatter | solution.py:156
Sparse Core Ops, SparseCore 0:
  28.0 231.7 all-gather.2
  553.4 234.6 all-gather.4
  794.3 137.5 reduce-scatter.1
